TPU v7x, 32 devices: a whole 2x2x4 slice. The times are simulated.
32 devices in a mesh: tile: 16 (over z, x, core), wave: 2 (over y).
Axes of the slice: x: 2, y: 2, z: 4, core: 2. Of those that a mesh axis runs over, the one named last changes fastest.
Arguments:
- params: float32 [9, 256, 128], P(None, 'tile'), may hold values from -6 to 6
- dual_in: float32 [2, 9, 256, 128], P(None, None, 'tile'), may hold values from -4 to 4
- jacobian: bfloat16 [4, 9, 256, 128], P(None, None, 'tile'), may hold values from -3 to 3
- response: float32 [9, 64], P(None, 'wave'), may hold values from -5 to 5
- observed: bfloat16 [4, 64, 256, 128], P(None, 'wave', 'tile'), may hold values from -6 to 6
- psf: bfloat16 [17, 17], replicated, may hold values from -0.375 to 0.375
- step_size: float32 [], replicated, may hold values from 0.03 to 0.06
- dual_step: float32 [], replicated, may hold values from 0.5 to 1
- tv_bound: float32 [], replicated, may hold values from 1 to 2
- clip_bound: float32 [], replicated, may hold values from 0.5 to 1
Outputs:
- params_out: float32 [9, 256, 128], P(None, 'tile')
- dual_out: float32 [2, 9, 256, 128], P(None, None, 'tile')
- misfit: float32 [], replicated
All inputs are finite; a program needn't handle non-finite values.
Results may differ from a plain program's by a relative error of at most 0.0033.
Values may be sent and summed in bfloat16 or wider, within the bound.
A program may use at most 128 MiB of HBM per device.

v0:
```python
import functools

import jax
import jax.numpy as jnp
from jax import lax
from jax.experimental import pallas as pl
from jax.experimental.pallas import tpu as pltpu
from jax.sharding import PartitionSpec as P

MESH = pl.DeviceIdType.MESH
HALO = 8
EDGE = 2 * HALO
TAPS = 17
PAIRS = 9
F32 = jnp.float32
BF16 = jnp.bfloat16


def split_hi_lo(value):
    high = value.astype(BF16).astype(F32)
    return high, value - high


def group_size(count):
    size = 1
    while size * size < count:
        size *= 2
    return size if count % size == 0 else count


def kernel(
    tiles, waves, total_count,
    params_h, dual_h, jac_h, obs_h, response, psf, step_size, dual_step, tv_bound, clip_bound,
    x_out, d_out_h, m_out,
    d_out, params, dual, jac, obs,
    mats, obs_f, jac_f, terms, pairs, proj, acc, xpad, dpad, base, respad, psfpad, rt, rbf, rtb,
    jac_edge, jac_up, jac_dn, par_up, par_dn, dual_up, div_edge, div_up, div_dn,
    full0, edge0, full1, edge1, full0_in, up0_in, dn0_in, full1_in, up1_in, dn1_in,
    m_own, m_mid, m_group, m_cross,
    local, in_send, in_recv, f_send, f_recv, u_send, u_recv, d_send, d_recv,
    mg_send, mg_recv, mc_send, mc_recv,
):
    npar, rows, ncol = params.shape
    images = jac.shape[0]
    stokes = images // npar
    nwave = response.shape[1]
    nimg = stokes * nwave
    width = -(-images // 8) * 8
    wide = -(-images // 16) * 16
    padded = rows + EDGE
    npair = padded // 2
    opair = rows // 2
    me_t = lax.axis_index("tile")
    me_w = lax.axis_index("wave")
    up = lax.rem(me_t + tiles - 1, tiles)
    down = lax.rem(me_t + 1, tiles)
    gsize = group_size(tiles)
    ngroup = tiles // gsize
    my_group = me_t // gsize
    my_place = lax.rem(me_t, gsize)
    spin = [me_w] + [lax.rem(me_w + d, waves) for d in range(1, waves)]
    group_tiles = [me_t]
    group_tiles += [my_group * gsize + lax.rem(my_place + d, gsize) for d in range(1, gsize)]
    group_peers = [(t, w) for i, t in enumerate(group_tiles) for j, w in enumerate(spin) if i + j > 0]
    cross_peers = [
        (lax.rem(my_group + d, ngroup) * gsize + my_place, me_w) for d in range(1, ngroup)
    ]

    barrier = pltpu.get_barrier_semaphore()
    peers = [(t, w) for w in spin for t in (up, down)] + group_peers + cross_peers
    for peer in peers:
        pl.semaphore_signal(barrier, inc=1, device_id=peer, device_id_type=MESH)
    fetch = [
        pltpu.make_async_copy(jac_h, jac, local.at[0]),
        pltpu.make_async_copy(params_h, params, local.at[1]),
        pltpu.make_async_copy(dual_h, dual, local.at[2]),
        pltpu.make_async_copy(obs_h, obs, local.at[3]),
    ]
    for copy in fetch:
        copy.start()
    fetch[0].wait()
    for m in range(images):
        jac_f[m, HALO:HALO + rows, :] = jac[m].astype(F32)
    jac_edge[0] = jac_f[:, HALO:EDGE, :].reshape(images * HALO, ncol).astype(BF16)
    jac_edge[1] = jac_f[:, rows:rows + HALO, :].reshape(images * HALO, ncol).astype(BF16)
    fetch[1].wait()
    fetch[2].wait()
    pl.semaphore_wait(barrier, len(peers))

    def remote(src, dst, send, recv, peer):
        return pltpu.make_async_remote_copy(
            src_ref=src, dst_ref=dst, send_sem=send, recv_sem=recv,
            device_id=peer, device_id_type=MESH,
        )

    above, below = (up, me_w), (down, me_w)
    first = [
        remote(params.at[:, pl.ds(rows - HALO, HALO)], par_up, in_send.at[0], in_recv.at[0], below),
        remote(params.at[:, pl.ds(0, HALO)], par_dn, in_send.at[1], in_recv.at[1], above),
        remote(dual.at[0, :, pl.ds(rows - HALO, HALO)], dual_up, in_send.at[2], in_recv.at[2], below),
        remote(jac_edge.at[1], jac_up, in_send.at[3], in_recv.at[3], below),
        remote(jac_edge.at[0], jac_dn, in_send.at[4], in_recv.at[4], above),
    ]
    for copy in first:
        copy.start()

    step = step_size[0]
    clip = clip_bound[0]
    bound = tv_bound[0]
    dstep = dual_step[0]

    zero_block = jnp.zeros((ncol, ncol), BF16)
    mats[0, ncol:, 0:ncol] = zero_block
    mats[PAIRS - 1, 0:ncol, ncol:] = zero_block
    psfpad[...] = jnp.zeros_like(psfpad)
    psfpad[0:TAPS, 0:TAPS] = psf[...].astype(F32)
    taps = pltpu.roll(psfpad[...], ncol - HALO, 1)
    for tap in range(TAPS):
        line = jnp.broadcast_to(taps[tap:tap + 1, :], (ncol, ncol))
        block = pltpu.roll(line, 0, 1, stride=1, stride_axis=0).astype(BF16)
        if tap % 2 == 0:
            mats[tap // 2, 0:ncol, 0:ncol] = block
            mats[tap // 2, ncol:, ncol:] = block
        else:
            mats[tap // 2, 0:ncol, ncol:] = block
            mats[tap // 2 + 1, ncol:, 0:ncol] = block

    respad[...] = jnp.zeros_like(respad)
    respad[0:npar, 0:nwave] = response[...]
    rt[...] = jnp.zeros_like(rt)
    spread = respad[...]
    for s in range(stokes):
        shifted = spread if s == 0 else pltpu.roll(spread, s * nwave, 1)
        for part in range(3):
            at = part * width + s * npar
            rt[at:at + npar, :] = shifted[0:npar]
    full = rt[...]
    high, low = split_hi_lo(full)
    place = lax.broadcasted_iota(jnp.int32, full.shape, 0)
    rbf[...] = jnp.where(place < 2 * width, high, low).T.astype(BF16)
    rtb[...] = jnp.concatenate([high[0:width], low[0:width]], axis=0).astype(BF16)

    for m in range(images, width):
        terms[m * padded:(m + 1) * padded, :] = jnp.zeros((padded, ncol), F32)
    d1 = params[...]
    xpad[:, HALO:HALO + rows, :] = d1
    d1 = pltpu.roll(d1, ncol - 1, 2) - d1
    d1 = jnp.clip(dual[1] + dstep * d1, -bound, bound)
    d_out[1] = d1
    fetch[3].wait()
    obs_f[...] = obs[...].astype(F32).reshape(nimg * rows, ncol)

    for copy in first:
        copy.wait()
    xpad[:, 0:HALO, :] = par_up[...]
    xpad[:, HALO + rows:, :] = par_dn[...]
    d0 = xpad[:, HALO + 1:HALO + 1 + rows, :] - xpad[:, HALO:HALO + rows, :]
    d0 = jnp.clip(dual[0] + dstep * d0, -bound, bound)
    d_out[0] = d0
    side = xpad[:, 1:HALO + 1, :] - xpad[:, 0:HALO, :]
    dpad[:, 0:HALO, :] = jnp.clip(dual_up[...] + dstep * side, -bound, bound)
    dpad[:, HALO:, :] = d0
    div = (d0 - dpad[:, HALO - 1:HALO - 1 + rows, :]) + (d1 - pltpu.roll(d1, 1, 2))
    base[:, HALO:HALO + rows, :] = div
    div_edge[0] = div[:, 0:HALO, :]
    div_edge[1] = div[:, rows - HALO:, :]
    copies_v = [
        remote(div_edge.at[1], div_up, in_send.at[5], in_recv.at[5], below),
        remote(div_edge.at[0], div_dn, in_send.at[6], in_recv.at[6], above),
    ]
    for copy in copies_v:
        copy.start()
    jac_f[:, 0:HALO, :] = jac_up[...].astype(F32).reshape(images, HALO, ncol)
    jac_f[:, HALO + rows:, :] = jac_dn[...].astype(F32).reshape(images, HALO, ncol)

    keep = pltpu.make_async_copy(d_out, d_out_h, local.at[4])
    keep.start()
    zero_k = jnp.zeros((rbf.shape[1] - 3 * width, 2 * ncol), F32)

    def widen(value):
        if wide == width:
            return value.astype(BF16)
        fill = jnp.zeros((wide - width, value.shape[1]), F32)
        return jnp.concatenate([value, fill], axis=0).astype(BF16)

    for it in range(2):
        for m in range(images):
            terms[m * padded:(m + 1) * padded, :] = jac_f[m] * xpad[m % npar]
        for q in range(npair):
            for i in range(2):
                value = terms[pl.ds(2 * q + i, width, stride=padded), :]
                value = jnp.concatenate(split_hi_lo(value), axis=0).astype(BF16)
                pairs[q * 2 * width:(q + 1) * 2 * width, i * ncol:(i + 1) * ncol] = value
        total = None
        for k in range(PAIRS):
            window = pairs[k * 2 * width:(k + opair) * 2 * width, :]
            part = lax.dot_general(
                window, mats[k], (((1,), (1,)), ((), ())), preferred_element_type=F32
            )
            total = part if total is None else total + part
        loss = jnp.zeros((8, ncol), F32)
        for r in range(opair):
            both = total[r * 2 * width:(r + 1) * 2 * width]
            bhi, blo = split_hi_lo(both[:width] + both[width:])
            stack = jnp.concatenate([bhi, blo, bhi, zero_k], axis=0).astype(BF16)
            blurred = jnp.dot(rbf[...], stack, preferred_element_type=F32)
            halves = []
            for i in range(2):
                target = obs_f[pl.ds(2 * r + i, nimg, stride=rows), :]
                resid = blurred[:, i * ncol:(i + 1) * ncol] - target
                held = jnp.clip(resid, -clip, clip)
                if it == 0:
                    huber = held * (resid - 0.5 * held)
                    loss = loss + jnp.sum(huber.reshape(nimg // 8, 8, ncol), axis=0)
                halves.append(held.astype(BF16))
            weighted = jnp.concatenate(halves, axis=1)
            both = jnp.dot(rtb[...], weighted, preferred_element_type=F32)
            proj[r * wide:(r + 1) * wide, :] = widen(both[:width] + both[width:])
        if it == 0:
            m_own[...] = loss
            slot = my_place * waves + me_w
            m_group[slot] = loss
            copies_g = [
                remote(m_own, m_group.at[slot], mg_send.at[d], mg_recv.at[d], peer)
                for d, peer in enumerate(group_peers)
            ]
            for copy in copies_g:
                copy.start()
        for k in range(PAIRS):
            back = jnp.dot(proj[...], mats[k], preferred_element_type=F32)
            for q in range(opair):
                part = back[q * wide:(q + 1) * wide]
                at = (k + q) * wide
                if k == 0 or q == opair - 1:
                    acc[at:at + wide, :] = part
                else:
                    acc[at:at + wide, :] += part
        for q in range(npair):
            for i in range(2):
                value = acc[q * wide:q * wide + width, i * ncol:(i + 1) * ncol]
                terms[pl.ds(2 * q + i, width, stride=padded), :] = value
        grads = []
        for p in range(npar):
            grad = None
            for s in range(stokes):
                m = s * npar + p
                part = jac_f[m] * terms[m * padded:(m + 1) * padded, :]
                grad = part if grad is None else grad + part
            grads.append(grad)
        reach = EDGE if it == 0 else HALO
        whole = grads if it == 0 else [g[HALO:HALO + rows] for g in grads]
        whole = jnp.concatenate(whole, axis=0).astype(BF16)
        full_out, edge_out = (full0, edge0) if it == 0 else (full1, edge1)
        full_in, up_in, dn_in = (full0_in, up0_in, dn0_in) if it == 0 else (full1_in, up1_in, dn1_in)
        edge_out[0] = jnp.concatenate([g[:reach] for g in grads], axis=0).astype(BF16)
        edge_out[1] = jnp.concatenate([g[padded - reach:] for g in grads], axis=0).astype(BF16)
        full_out[...] = whole
        full_in[me_w] = whole
        copies = []
        for d in range(waves - 1, -1, -1):
            copies += [
                remote(edge_out.at[1], up_in.at[me_w], u_send.at[it, d], u_recv.at[it, d], (down, spin[d])),
                remote(edge_out.at[0], dn_in.at[me_w], d_send.at[it, d], d_recv.at[it, d], (up, spin[d])),
            ]
        for d in range(1, waves):
            copies.append(
                remote(full_out, full_in.at[me_w], f_send.at[it, d], f_recv.at[it, d], (me_t, spin[d]))
            )
        for copy in copies:
            copy.start()
        if it == 0:
            for copy in copies_v:
                copy.wait()
            base[:, 0:HALO, :] = div_up[...]
            base[:, HALO + rows:, :] = div_dn[...]
            base[...] = xpad[...] + step * base[...]
        for copy in copies:
            copy.wait()

        def added(ref, count):
            value = ref[0].astype(F32)
            for w in range(1, waves):
                value = value + ref[w].astype(F32)
            return value.reshape(npar, count, ncol)

        span = padded if it == 0 else rows
        inner = added(full_in, span)
        top = inner[:, :reach] + added(up_in, reach)
        low = inner[:, span - reach:] + added(dn_in, reach)
        if it == 0:
            kept = [base[:, :reach, :] - step * top]
            if span > 2 * reach:
                kept.append(base[:, reach:span - reach, :] - step * inner[:, reach:span - reach])
            kept.append(base[:, span - reach:, :] - step * low)
            mid = base[:, HALO:HALO + rows, :] - xpad[:, HALO:HALO + rows, :]
            at = 0
            for value in kept:
                xpad[:, at:at + value.shape[1], :] = value
                at += value.shape[1]
            base[:, HALO:HALO + rows, :] = xpad[:, HALO:HALO + rows, :] + mid
            for copy in copies_g:
                copy.wait()
            total_m = m_group[0]
            for g in range(1, gsize * waves):
                total_m = total_m + m_group[g]
            m_mid[...] = total_m
            m_cross[my_group] = total_m
            copies_c = [
                remote(m_mid, m_cross.at[my_group], mc_send.at[d], mc_recv.at[d], peer)
                for d, peer in enumerate(cross_peers)
            ]
            for copy in copies_c:
                copy.start()
        else:
            x_out[:, 0:reach, :] = base[:, HALO:HALO + reach, :] - step * top
            if span > 2 * reach:
                x_out[:, reach:span - reach, :] = (
                    base[:, HALO + reach:HALO + span - reach, :] - step * inner[:, reach:span - reach]
                )
            x_out[:, span - reach:, :] = base[:, HALO + span - reach:HALO + span, :] - step * low
            for copy in copies_c + [keep]:
                copy.wait()
            tot = m_cross[0]
            for g in range(1, ngroup):
                tot = tot + m_cross[g]
            m_out[0] = jnp.sum(tot) / total_count


def per_device(
    params, dual_in, jacobian, response, observed, psf, step_size, dual_step, tv_bound, clip_bound
):
    stokes, nwave, rows, ncol = observed.shape
    npar = params.shape[0]
    nimg = stokes * nwave
    images = stokes * npar
    width = -(-images // 8) * 8
    wide = -(-images // 16) * 16
    kdim = -(-3 * width // 128) * 128
    padded = rows + EDGE
    npair = padded // 2
    opair = rows // 2
    tiles = lax.axis_size("tile")
    waves = lax.axis_size("wave")
    total_count = float(nimg * waves * rows * tiles * ncol)
    gsize = group_size(tiles)
    ngroup = tiles // gsize
    vmem = pl.BlockSpec(memory_space=pltpu.VMEM)
    smem = pl.BlockSpec(memory_space=pltpu.SMEM)
    hbm = pl.BlockSpec(memory_space=pltpu.HBM)
    dma = pltpu.SemaphoreType.DMA
    state, dual_out, misfit = pl.pallas_call(
        functools.partial(kernel, tiles, waves, total_count),
        out_shape=(
            jax.ShapeDtypeStruct((npar, rows, ncol), F32),
            jax.ShapeDtypeStruct((2, npar, rows, ncol), F32),
            jax.ShapeDtypeStruct((1,), F32),
        ),
        in_specs=[hbm] * 4 + [vmem] * 2 + [smem] * 4,
        out_specs=(vmem, hbm, smem),
        scratch_shapes=[
            pltpu.VMEM((2, npar, rows, ncol), F32),
            pltpu.VMEM((npar, rows, ncol), F32),
            pltpu.VMEM((2, npar, rows, ncol), F32),
            pltpu.VMEM((images, rows, ncol), BF16),
            pltpu.VMEM((nimg, rows, ncol), BF16),
            pltpu.VMEM((PAIRS, 2 * ncol, 2 * ncol), BF16),
            pltpu.VMEM((nimg * rows, ncol), F32),
            pltpu.VMEM((images, padded, ncol), F32),
            pltpu.VMEM((width * padded, ncol), F32),
            pltpu.VMEM((npair * 2 * width, 2 * ncol), BF16),
            pltpu.VMEM((opair * wide, 2 * ncol), BF16),
            pltpu.VMEM((npair * wide, 2 * ncol), F32),
            pltpu.VMEM((npar, padded, ncol), F32),
            pltpu.VMEM((npar, rows + HALO, ncol), F32),
            pltpu.VMEM((npar, padded, ncol), F32),
            pltpu.VMEM((-(-npar // 8) * 8, nimg), F32),
            pltpu.VMEM((-(-TAPS // 8) * 8, ncol), F32),
            pltpu.VMEM((kdim, nimg), F32),
            pltpu.VMEM((nimg, kdim), BF16),
            pltpu.VMEM((2 * width, nimg), BF16),
            pltpu.VMEM((2, images * HALO, ncol), BF16),
            pltpu.VMEM((images * HALO, ncol), BF16),
            pltpu.VMEM((images * HALO, ncol), BF16),
            pltpu.VMEM((npar, HALO, ncol), F32),
            pltpu.VMEM((npar, HALO, ncol), F32),
            pltpu.VMEM((npar, HALO, ncol), F32),
            pltpu.VMEM((2, npar, HALO, ncol), F32),
            pltpu.VMEM((npar, HALO, ncol), F32),
            pltpu.VMEM((npar, HALO, ncol), F32),
            pltpu.VMEM((npar * padded, ncol), BF16),
            pltpu.VMEM((2, npar * EDGE, ncol), BF16),
            pltpu.VMEM((npar * rows, ncol), BF16),
            pltpu.VMEM((2, npar * HALO, ncol), BF16),
            pltpu.VMEM((waves, npar * padded, ncol), BF16),
            pltpu.VMEM((waves, npar * EDGE, ncol), BF16),
            pltpu.VMEM((waves, npar * EDGE, ncol), BF16),
            pltpu.VMEM((waves, npar * rows, ncol), BF16),
            pltpu.VMEM((waves, npar * HALO, ncol), BF16),
            pltpu.VMEM((waves, npar * HALO, ncol), BF16),
            pltpu.VMEM((8, ncol), F32),
            pltpu.VMEM((8, ncol), F32),
            pltpu.VMEM((gsize * waves, 8, ncol), F32),
            pltpu.VMEM((ngroup, 8, ncol), F32),
            dma((5,)),
            dma((7,)), dma((7,)),
            dma((2, waves)), dma((2, waves)),
            dma((2, waves)), dma((2, waves)),
            dma((2, waves)), dma((2, waves)),
            dma((gsize * waves,)), dma((gsize * waves,)),
            dma((ngroup,)), dma((ngroup,)),
        ],
        compiler_params=pltpu.CompilerParams(
            collective_id=0, has_side_effects=True, vmem_limit_bytes=66_000_000
        ),
    )(
        params, dual_in, jacobian.reshape(images, rows, ncol),
        observed.reshape(nimg, rows, ncol), response, psf,
        step_size.reshape(1), dual_step.reshape(1), tv_bound.reshape(1), clip_bound.reshape(1),
    )
    return state, dual_out, misfit.reshape(())


def solution(mesh):
    in_specs = (
        P(None, "tile", None),
        P(None, None, "tile", None),
        P(None, None, "tile", None),
        P(None, "wave"),
        P(None, "wave", "tile", None),
        P(),
        P(),
        P(),
        P(),
        P(),
    )
    out_specs = (P(None, "tile", None), P(None, None, "tile", None), P())
    return jax.shard_map(
        per_device, mesh=mesh, in_specs=in_specs, out_specs=out_specs, check_vma=False
    )
```

profile of v0, /device:TPU:0, one launch (start us, length us, event | category | flops | bytes accessed | tf_op | source)
XLA Modules:
  0.0 37.0 jit_solution(14840823134174469831)
XLA Ops:
  3.2 29.8 %shard_map.121 = (f32[9,16,128]{2,1,0:T(8,128)}, f32[2,9,16,128]{3,2,1,0:T(8,128)}, f32[1]{0:T(128)}) custom-call(f32[9,16,128]{2,1,0:T(8,128)} %params_h.1, f32[2,9,16,128]{3,2,1,0:T(8,128)} %dual_h.1, bf16[36,16,128]{2,1,0:T(8,128)(2,1)} %bitcast.12, bf16[128,16,128]{2,1,0:T(8,128)(2,1)} %bitcast.11, f32[9,32]{1,0:T(8,128)} %response.1, ...), custom_call_target="tpu_custom_call" | custom-call | tf_op jit(solution)/shard_map/pallas_call | solution.py:351
  33.0 0.0 copy-start
  33.0 1.6 %copy.20 = f32[9,16,128]{2,1,0:T(8,128)} copy(f32[9,16,128]{2,1,0:T(8,128)} %get-tuple-element.12) | data formatting | bytes 147456
  34.6 0.0 copy-done
  34.6 0.7 %copy.21 = f32[2,9,16,128]{3,2,1,0:T(8,128)} copy(f32[2,9,16,128]{3,2,1,0:T(8,128)S(1)} %copy-done) | data formatting | bytes 294912
Async XLA Ops:
  33.0 1.6 %copy-start = (f32[2,9,16,128]{3,2,1,0:T(8,128)S(1)}, f32[2,9,16,128]{3,2,1,0:T(8,128)}, u32[]{:S(2)}) copy-start(f32[2,9,16,128]{3,2,1,0:T(8,128)} %get-tuple-element.13) | copy-start | bytes 442372
where the time goes:
time: 37.3 us; the launch traced here: 37 us
  Pallas kernels  29.8 us (80%)
  between operations  5 us (13%)
  local copies, waits for them, and re-layouts  2.22 us (6%)
    pallas_call x1, Pallas kernels, per_device(): pl.pallas_call(functools.partial(kernel, tiles, waves, total_count), out_...  29.8 us
    unnamed x4, local copies, waits for them, and re-layouts  2.22 us

commit v1 on v0

--- a/solution.py
+++ b/solution.py
@@ -31,8 +31,8 @@
 def kernel(
     tiles, waves, total_count,
     params_h, dual_h, jac_h, obs_h, response, psf, step_size, dual_step, tv_bound, clip_bound,
-    x_out, d_out_h, m_out,
-    d_out, params, dual, jac, obs,
+    x_out, d_out, m_out,
+    params, dual, jac, obs,
     mats, obs_f, jac_f, terms, pairs, proj, acc, xpad, dpad, base, respad, psfpad, rt, rbf, rtb,
     jac_edge, jac_up, jac_dn, par_up, par_dn, dual_up, div_edge, div_up, div_dn,
     full0, edge0, full1, edge1, full0_in, up0_in, dn0_in, full1_in, up1_in, dn1_in,
@@ -173,8 +173,6 @@
     jac_f[:, 0:HALO, :] = jac_up[...].astype(F32).reshape(images, HALO, ncol)
     jac_f[:, HALO + rows:, :] = jac_dn[...].astype(F32).reshape(images, HALO, ncol)
 
-    keep = pltpu.make_async_copy(d_out, d_out_h, local.at[4])
-    keep.start()
     zero_k = jnp.zeros((rbf.shape[1] - 3 * width, 2 * ncol), F32)
 
     def widen(value):
@@ -318,12 +316,21 @@
                     base[:, HALO + reach:HALO + span - reach, :] - step * inner[:, reach:span - reach]
                 )
             x_out[:, span - reach:, :] = base[:, HALO + span - reach:HALO + span, :] - step * low
-            for copy in copies_c + [keep]:
+            for copy in copies_c:
                 copy.wait()
             tot = m_cross[0]
             for g in range(1, ngroup):
                 tot = tot + m_cross[g]
-            m_out[0] = jnp.sum(tot) / total_count
+            m_out[...] = jnp.full((8, ncol), jnp.sum(tot) / total_count, F32)
+
+
+def hand_out(x, d, m, x_h, d_h, m_s, sem):
+    copies = [pltpu.make_async_copy(x, x_h, sem.at[0]), pltpu.make_async_copy(d, d_h, sem.at[1])]
+    for copy in copies:
+        copy.start()
+    m_s[0] = m[0, 0]
+    for copy in copies:
+        copy.wait()
 
 
 def per_device(
@@ -351,14 +358,13 @@
     state, dual_out, misfit = pl.pallas_call(
         functools.partial(kernel, tiles, waves, total_count),
         out_shape=(
-            jax.ShapeDtypeStruct((npar, rows, ncol), F32),
-            jax.ShapeDtypeStruct((2, npar, rows, ncol), F32),
-            jax.ShapeDtypeStruct((1,), F32),
+            pltpu.VMEM((npar, rows, ncol), F32),
+            pltpu.VMEM((2, npar, rows, ncol), F32),
+            pltpu.VMEM((8, ncol), F32),
         ),
         in_specs=[hbm] * 4 + [vmem] * 2 + [smem] * 4,
-        out_specs=(vmem, hbm, smem),
+        out_specs=(vmem, vmem, vmem),
         scratch_shapes=[
-            pltpu.VMEM((2, npar, rows, ncol), F32),
             pltpu.VMEM((npar, rows, ncol), F32),
             pltpu.VMEM((2, npar, rows, ncol), F32),
             pltpu.VMEM((images, rows, ncol), BF16),
@@ -417,6 +423,18 @@
         observed.reshape(nimg, rows, ncol), response, psf,
         step_size.reshape(1), dual_step.reshape(1), tv_bound.reshape(1), clip_bound.reshape(1),
     )
+    state, dual_out, misfit = pl.pallas_call(
+        hand_out,
+        out_shape=(
+            jax.ShapeDtypeStruct((npar, rows, ncol), F32),
+            jax.ShapeDtypeStruct((2, npar, rows, ncol), F32),
+            jax.ShapeDtypeStruct((1,), F32),
+        ),
+        in_specs=[vmem] * 3,
+        out_specs=(hbm, hbm, smem),
+        scratch_shapes=[dma((2,))],
+        compiler_params=pltpu.CompilerParams(vmem_limit_bytes=1_000_000),
+    )(state, dual_out, misfit)
     return state, dual_out, misfit.reshape(())
 
 

time: 37.3 us -> 34 us (0.912)
  local copies, waits for them, and re-layouts: 2.22 us -> 0 us
  between operations: 5 us -> 3.22 us
  Pallas kernels: 29.8 us -> 30.5 us
    unnamed x4 -> x0, local copies, waits for them, and re-layouts: 2.22 us -> none
    pallas_call x0 -> x1, Pallas kernels: none -> 1.22 us  [per_device(): pl.pallas_call(hand_out, out_shape=(jax.ShapeDtypeStruct((npar, rows, nco...]
    pallas_call x1, Pallas kernels: 29.8 us -> 29.3 us  [per_device(): pl.pallas_call(functools.partial(kernel, tiles, waves, total_count), out_...]
where the time goes in v1:
time: 34 us; the launch traced here: 33.7 us
  Pallas kernels  30.5 us (90%)
  between operations  3.22 us (9%)
    pallas_call x1, Pallas kernels, per_device(): pl.pallas_call(functools.partial(kernel, tiles, waves, total_count), out_...  29.3 us
    pallas_call x1, Pallas kernels, per_device(): pl.pallas_call(hand_out, out_shape=(jax.ShapeDtypeStruct((npar, rows, nco...  1.22 us

profile of v1, /device:TPU:0, one launch (start us, length us, event | category | flops | bytes accessed | tf_op | source)
XLA Modules:
  0.0 33.7 jit_solution(11850217540159351330)
XLA Ops:
  3.2 29.3 %shard_map.121 = (f32[9,16,128]{2,1,0:T(8,128)S(1)}, f32[2,9,16,128]{3,2,1,0:T(8,128)S(1)}, f32[8,128]{1,0:T(8,128)S(1)}) custom-call(f32[9,16,128]{2,1,0:T(8,128)} %params_h.1, f32[2,9,16,128]{3,2,1,0:T(8,128)} %dual_h.1, bf16[36,16,128]{2,1,0:T(8,128)(2,1)} %bitcast.12, bf16[128,16,128]{2,1,0:T(8,128)(2,1)} %bitcast.11, f32[9,32]{1,0:T(8,128)} %response.1, ...), custom_call_target="tpu_custom_call" | custom-call | tf_op jit(solution)/shard_map/pallas_call | solution.py:358
  32.5 1.2 %shard_map.122 = (f32[9,16,128]{2,1,0:T(8,128)}, f32[2,9,16,128]{3,2,1,0:T(8,128)}, f32[1]{0:T(128)}) custom-call(f32[9,16,128]{2,1,0:T(8,128)S(1)} %get-tuple-element.9.x, f32[2,9,16,128]{3,2,1,0:T(8,128)S(1)} %get-tuple-element.10.d, f32[8,128]{1,0:T(8,128)S(1)} %get-tuple-element.11.m), custom_call_target="tpu_custom_call" | custom-call | tf_op jit(solution)/shard_map/pallas_call | solution.py:426

commit v2 on v1

v2 whole, which is shorter than its diff:
```python
import functools

import jax
import jax.numpy as jnp
from jax import lax
from jax.experimental import pallas as pl
from jax.experimental.pallas import tpu as pltpu
from jax.sharding import PartitionSpec as P

MESH = pl.DeviceIdType.MESH
HALO = 8
TAPS = 17
F32 = jnp.float32
BF16 = jnp.bfloat16


def split_hi_lo(value):
    high = value.astype(BF16).astype(F32)
    return high, value - high


def group_size(count):
    size = 1
    while size * size < count:
        size *= 2
    return size if count % size == 0 else count


def kernel(
    tiles, waves, total_count,
    params_h, dual_h, jac_h, obs_h, response, psf, step_size, dual_step, tv_bound, clip_bound,
    x_out, d_out, m_out,
    params, dual, jac, obs,
    wt, main_a, half_a, obs_f, obs_l, jac_n, jac_l, x_l, lhs, tot, proj, prod, grad_c,
    x_c, div_c, base_c, div_n, dpad, respad, psfpad, rt, rbf, rtb,
    jac_edge, jac_up, jac_dn, row_dn, row_up, row_above, row_below,
    full0, edge0, full1, edge1, full0_in, up0_in, dn0_in, full1_in, up1_in, dn1_in,
    m_own, m_mid, m_group, m_cross,
    local, in_send, in_recv, f_send, f_recv, u_send, u_recv, d_send, d_recv,
    mg_send, mg_recv, mc_send, mc_recv,
):
    npar, rows, ncol = params.shape
    images = jac.shape[0]
    stokes = images // npar
    nwave = response.shape[1]
    nimg = stokes * nwave
    width = -(-images // 8) * 8
    wide = -(-images // 16) * 16
    nrg = rows // HALO
    span = nrg + 2
    blk = HALO
    cols = ncol // blk
    unit = npar * blk
    half_rows = 16 * -(-npar // 16)
    me_t = lax.axis_index("tile")
    me_w = lax.axis_index("wave")
    up = lax.rem(me_t + tiles - 1, tiles)
    down = lax.rem(me_t + 1, tiles)
    gsize = group_size(tiles)
    ngroup = tiles // gsize
    my_group = me_t // gsize
    my_place = lax.rem(me_t, gsize)
    spin = [me_w] + [lax.rem(me_w + d, waves) for d in range(1, waves)]
    group_tiles = [me_t]
    group_tiles += [my_group * gsize + lax.rem(my_place + d, gsize) for d in range(1, gsize)]
    group_peers = [(t, w) for i, t in enumerate(group_tiles) for j, w in enumerate(spin) if i + j > 0]
    cross_peers = [
        (lax.rem(my_group + d, ngroup) * gsize + my_place, me_w) for d in range(1, ngroup)
    ]

    barrier = pltpu.get_barrier_semaphore()
    peers = [(up, me_w), (down, me_w)] + group_peers + cross_peers
    for peer in peers:
        pl.semaphore_signal(barrier, inc=1, device_id=peer, device_id_type=MESH)
    fetch = [
        pltpu.make_async_copy(jac_h, jac, local.at[0]),
        pltpu.make_async_copy(params_h, params, local.at[1]),
        pltpu.make_async_copy(dual_h, dual, local.at[2]),
        pltpu.make_async_copy(obs_h, obs, local.at[3]),
    ]
    for copy in fetch:
        copy.start()

    lane = lax.broadcasted_iota(jnp.int32, (1, ncol), 1)
    group_bit = [(lane // (cols << b)) % 2 == 0 for b in range(3)]
    near = lane % cols < HALO

    def swap_blocks(parts):
        parts = list(parts)
        for b in range(3):
            k = 1 << b
            shift = cols * k
            for i in range(blk):
                if i & k:
                    continue
                one, two = parts[i], parts[i + k]
                parts[i] = jnp.where(group_bit[b], one, pltpu.roll(two, shift, 1))
                parts[i + k] = jnp.where(group_bit[b], pltpu.roll(one, ncol - shift, 1), two)
        return parts

    def image_rows(rg, b):
        return slice((rg * blk + b) * width, (rg * blk + b + 1) * width)

    def unit_rows(rg, b):
        return slice((rg * blk + b) * npar, (rg * blk + b + 1) * npar)

    def to_units(source, target, rg_from, rg_to):
        parts = swap_blocks([source[:, rg_from * HALO + r, :] for r in range(HALO)])
        for b in range(blk):
            target[unit_rows(rg_to, b), :] = parts[b]

    jac_n[images * rows:, :] = jnp.zeros((jac_n.shape[0] - images * rows, ncol), F32)
    fetch[0].wait()
    for m in range(images):
        jac_n[m * rows:(m + 1) * rows, :] = jac[m].astype(F32)
    for rg in range(nrg):
        for g in range(width // 8):
            parts = swap_blocks(
                [jac_n[pl.ds(g * 8 * rows + rg * HALO + r, 8, stride=rows), :] for r in range(HALO)]
            )
            for b in range(blk):
                at = ((rg + 1) * blk + b) * width + g * 8
                jac_l[at:at + 8, :] = parts[b]
    jac_edge[0] = jac_l[blk * width:2 * blk * width, :].astype(BF16)
    jac_edge[1] = jac_l[nrg * blk * width:(nrg + 1) * blk * width, :].astype(BF16)
    fetch[1].wait()
    for rg in range(nrg):
        to_units(params, x_c, rg, rg + 1)
    fetch[2].wait()
    row_dn[...] = jnp.zeros_like(row_dn)
    row_up[...] = jnp.zeros_like(row_up)
    row_dn[0:npar, :] = params[:, rows - 1, :]
    row_dn[half_rows:half_rows + npar, :] = dual[0, :, rows - 1, :]
    row_up[0:npar, :] = params[:, 0, :]
    pl.semaphore_wait(barrier, len(peers))

    def remote(src, dst, send, recv, peer):
        return pltpu.make_async_remote_copy(
            src_ref=src, dst_ref=dst, send_sem=send, recv_sem=recv,
            device_id=peer, device_id_type=MESH,
        )

    above, below = (up, me_w), (down, me_w)

    def unit_span(rg, count):
        return pl.ds(rg * unit, count * unit)

    first = [
        remote(row_dn, row_above, in_send.at[0], in_recv.at[0], below),
        remote(row_up, row_below, in_send.at[1], in_recv.at[1], above),
        remote(jac_edge.at[1], jac_up, in_send.at[2], in_recv.at[2], below),
        remote(jac_edge.at[0], jac_dn, in_send.at[3], in_recv.at[3], above),
        remote(x_c.at[unit_span(nrg, 1)], x_c.at[unit_span(0, 1)], in_send.at[4], in_recv.at[4], below),
        remote(x_c.at[unit_span(1, 1)], x_c.at[unit_span(nrg + 1, 1)], in_send.at[5], in_recv.at[5], above),
    ]
    for copy in first:
        copy.start()

    step = step_size[0]
    clip = clip_bound[0]
    bound = tv_bound[0]
    dstep = dual_step[0]

    psfpad[...] = jnp.zeros_like(psfpad)
    psfpad[0:TAPS, 0:TAPS] = psf[...].astype(F32)
    taps = pltpu.roll(psfpad[...], ncol - HALO, 1)
    for tap in range(TAPS):
        line = jnp.broadcast_to(taps[tap:tap + 1, :], (cols, ncol))
        line = pltpu.roll(line, 0, 1, stride=1, stride_axis=0)
        side = jnp.where(near, pltpu.roll(line, ncol - cols, 1), pltpu.roll(line, cols, 1))
        for ref, value in ((main_a, line), (half_a, side)):
            value = jnp.where(lane < cols, value, 0.0)
            for b in range(3):
                value = value + pltpu.roll(value, cols << b, 1)
            ref[tap * cols:(tap + 1) * cols, :] = value
    edge1[...] = jnp.zeros_like(edge1)
    wt[0, ncol:, :] = jnp.zeros((wt.shape[1] - ncol, 2 * ncol), BF16)
    for rg in range(1, span):
        for ro in range(nrg):
            if not 0 <= rg - ro <= 2:
                wt[rg, ro * ncol:(ro + 1) * ncol, :] = jnp.zeros((ncol, 2 * ncol), BF16)
    for delta in range(3):
        for r in range(HALO):
            for part, ref in ((0, main_a), (1, half_a)):
                value = jnp.zeros((cols, ncol), F32)
                for kr in range(HALO):
                    tap = delta * HALO + kr - r
                    if 0 <= tap < TAPS:
                        value = jnp.where(lane // cols == kr, ref[tap * cols:(tap + 1) * cols, :], value)
                value = value.astype(BF16)
                for ro in range(nrg):
                    at = ro * ncol + r * cols
                    wt[ro + delta, at:at + cols, part * ncol:(part + 1) * ncol] = value

    def expand(rg):
        for b in range(blk):
            value = x_c[unit_rows(rg, b), :]
            at = (rg * blk + b) * width
            for s in range(stokes):
                x_l[at + s * npar:at + (s + 1) * npar, :] = value

    def build(rg):
        terms = [jac_l[image_rows(rg, b), :] * x_l[image_rows(rg, b), :] for b in range(blk)]
        for b in range(blk):
            side = jnp.where(near, terms[(b + 1) % blk], terms[(b + blk - 1) % blk])
            at = (rg * blk + b) * 2 * width
            for part, value in ((0, terms[b]), (1, side)):
                value = jnp.concatenate(split_hi_lo(value), axis=0).astype(BF16)
                lhs[at:at + 2 * width, part * ncol:(part + 1) * ncol] = value

    def forward(rg):
        window = lhs[rg * blk * 2 * width:(rg + 1) * blk * 2 * width, :]
        return lax.dot_general(
            window, wt[rg], (((1,), (1,)), ((), ())), preferred_element_type=F32
        )

    if width > images:
        for rg in range(span):
            for b in range(blk):
                at = (rg * blk + b) * width
                x_l[at + images:at + width, :] = jnp.zeros((width - images, ncol), F32)
    for rg in range(1, nrg + 1):
        expand(rg)
        build(rg)
    own = None
    for rg in range(1, nrg + 1):
        part = forward(rg)
        own = part if own is None else own + part
    tot[...] = own

    respad[...] = jnp.zeros_like(respad)
    respad[0:npar, 0:nwave] = response[...]
    rt[...] = jnp.zeros_like(rt)
    spread = respad[...]
    for s in range(stokes):
        shifted = spread if s == 0 else pltpu.roll(spread, s * nwave, 1)
        for part in range(3):
            at = part * width + s * npar
            rt[at:at + npar, :] = shifted[0:npar]
    full = rt[...]
    high, low = split_hi_lo(full)
    place = lax.broadcasted_iota(jnp.int32, full.shape, 0)
    rbf[...] = jnp.where(place < 2 * width, high, low).T.astype(BF16)
    rtb[...] = jnp.concatenate([high[0:width], low[0:width]], axis=0).astype(BF16)

    d1 = params[...]
    d1 = pltpu.roll(d1, ncol - 1, 2) - d1
    d1 = jnp.clip(dual[1] + dstep * d1, -bound, bound)
    d_out[1] = d1
    fetch[3].wait()
    obs_f[...] = obs[...].astype(F32).reshape(nimg * rows, ncol)
    for g in range(nimg // 8):
        for rg in range(nrg):
            parts = swap_blocks(
                [obs_f[pl.ds(g * 8 * rows + rg * HALO + r, 8, stride=rows), :] for r in range(HALO)]
            )
            for b in range(blk):
                at = b * nimg + g * 8
                obs_l[at:at + 8, rg * ncol:(rg + 1) * ncol] = parts[b]

    for copy in first[:2]:
        copy.wait()
    now = params[...]
    dpad[:, HALO:HALO + rows, :] = now
    dpad[:, HALO + rows, :] = row_below[0:npar, :]
    d0 = dpad[:, HALO + 1:HALO + 1 + rows, :] - now
    d0 = jnp.clip(dual[0] + dstep * d0, -bound, bound)
    d_out[0] = d0
    side = params[:, 0, :] - row_above[0:npar, :]
    side = jnp.clip(row_above[half_rows:half_rows + npar, :] + dstep * side, -bound, bound)
    dpad[:, HALO - 1, :] = side
    dpad[:, HALO:HALO + rows, :] = d0
    div_n[...] = (d0 - dpad[:, HALO - 1:HALO - 1 + rows, :]) + (d1 - pltpu.roll(d1, 1, 2))
    for rg in range(nrg):
        to_units(div_n, div_c, rg, rg + 1)
    copies_v = [
        remote(div_c.at[unit_span(nrg, 1)], div_c.at[unit_span(0, 1)], in_send.at[6], in_recv.at[6], below),
        remote(div_c.at[unit_span(1, 1)], div_c.at[unit_span(nrg + 1, 1)], in_send.at[7], in_recv.at[7], above),
    ]
    for copy in copies_v:
        copy.start()
    for copy in first[2:]:
        copy.wait()
    jac_l[0:blk * width, :] = jac_up[...].astype(F32)
    jac_l[(nrg + 1) * blk * width:, :] = jac_dn[...].astype(F32)
    zero_k = jnp.zeros((rbf.shape[1] - 3 * width, nrg * ncol), F32)

    def widen(value):
        if wide == width:
            return value.astype(BF16)
        fill = jnp.zeros((wide - width, value.shape[1]), F32)
        return jnp.concatenate([value, fill], axis=0).astype(BF16)

    for it in range(2):
        for rg in (0, nrg + 1) if it == 0 else range(span):
            expand(rg)
            build(rg)
        if it == 0:
            total = tot[...] + forward(0) + forward(nrg + 1)
        else:
            total = None
            for rg in range(span):
                part = forward(rg)
                total = part if total is None else total + part
        loss = jnp.zeros((8, nrg * ncol), F32)
        for b in range(blk):
            both = total[b * 2 * width:(b + 1) * 2 * width]
            bhi, blo = split_hi_lo(both[:width] + both[width:])
            stack = jnp.concatenate([bhi, blo, bhi, zero_k], axis=0).astype(BF16)
            blurred = jnp.dot(rbf[...], stack, preferred_element_type=F32)
            resid = blurred - obs_l[b * nimg:(b + 1) * nimg, :]
            held = jnp.clip(resid, -clip, clip)
            if it == 0:
                huber = held * (resid - 0.5 * held)
                loss = loss + jnp.sum(huber.reshape(nimg // 8, 8, nrg * ncol), axis=0)
            both = jnp.dot(rtb[...], held.astype(BF16), preferred_element_type=F32)
            proj[b * wide:(b + 1) * wide, :] = widen(both[:width] + both[width:])
        if it == 0:
            loss = sum(loss[:, i * ncol:(i + 1) * ncol] for i in range(nrg))
            m_own[...] = loss
            slot = my_place * waves + me_w
            m_group[slot] = loss
            copies_g = [
                remote(m_own, m_group.at[slot], mg_send.at[d], mg_recv.at[d], peer)
                for d, peer in enumerate(group_peers)
            ]
            for copy in copies_g:
                copy.start()
        for rg in range(span):
            back = jnp.dot(proj[...], wt[rg], preferred_element_type=F32)
            mains = [back[b * wide:b * wide + width, 0:ncol] for b in range(blk)]
            sides = [back[b * wide:b * wide + width, ncol:] for b in range(blk)]
            for b in range(blk):
                along = mains[b] + jnp.where(near, sides[(b + blk - 1) % blk], sides[(b + 1) % blk])
                at = (rg * blk + b) * width
                prod[at:at + width, :] = jac_l[at:at + width, :] * along
                grad = None
                for s in range(stokes):
                    part = prod[at + s * npar:at + (s + 1) * npar, :]
                    grad = part if grad is None else grad + part
                grad_c[unit_rows(rg, b), :] = grad
        reach = 2 * unit if it == 0 else unit
        size = span * unit
        start = 0 if it == 0 else unit
        full_out, edge_out = (full0, edge0) if it == 0 else (full1, edge1)
        full_in, up_in, dn_in = (full0_in, up0_in, dn0_in) if it == 0 else (full1_in, up1_in, dn1_in)
        edge_out[0, 0:reach, :] = grad_c[0:reach, :].astype(BF16)
        edge_out[1, 0:reach, :] = grad_c[size - reach:, :].astype(BF16)
        whole = grad_c[start:size - start, :].astype(BF16)
        full_out[...] = whole
        full_in[me_w] = whole
        copies = []
        for d in range(waves - 1, -1, -1):
            copies += [
                remote(edge_out.at[1], up_in.at[me_w], u_send.at[it, d], u_recv.at[it, d], (down, spin[d])),
                remote(edge_out.at[0], dn_in.at[me_w], d_send.at[it, d], d_recv.at[it, d], (up, spin[d])),
            ]
        for d in range(1, waves):
            copies.append(
                remote(full_out, full_in.at[me_w], f_send.at[it, d], f_recv.at[it, d], (me_t, spin[d]))
            )
        for copy in copies:
            copy.start()
        if it == 0:
            for copy in copies_v:
                copy.wait()
            base_c[...] = x_c[...] + step * div_c[...]
        else:
            base_c[unit:size - unit, :] = x_c[unit:size - unit, :] + step * div_c[unit:size - unit, :]
            for copy in copies_g:
                copy.wait()
            total_m = m_group[0]
            for g in range(1, gsize * waves):
                total_m = total_m + m_group[g]
            m_mid[...] = total_m
            m_cross[my_group] = total_m
            copies_c = [
                remote(m_mid, m_cross.at[my_group], mc_send.at[d], mc_recv.at[d], peer)
                for d, peer in enumerate(cross_peers)
            ]
            for copy in copies_c:
                copy.start()
        for copy in copies:
            copy.wait()

        def added(ref, count):
            value = ref[0, 0:count, :].astype(F32)
            for w in range(1, waves):
                value = value + ref[w, 0:count, :].astype(F32)
            return value

        inner = added(full_in, size - 2 * start)
        top = inner[:reach] + added(up_in, reach)
        low = inner[size - 2 * start - reach:] + added(dn_in, reach)
        end = size - start
        x_c[start:start + reach, :] = base_c[start:start + reach, :] - step * top
        if end - start > 2 * reach:
            x_c[start + reach:end - reach, :] = (
                base_c[start + reach:end - reach, :] - step * inner[reach:end - start - reach]
            )
        x_c[end - reach:end, :] = base_c[end - reach:end, :] - step * low
    for rg in range(nrg):
        parts = swap_blocks([x_c[unit_rows(rg + 1, b), :] for b in range(blk)])
        for r in range(HALO):
            x_out[:, rg * HALO + r, :] = parts[r]
    for copy in copies_c:
        copy.wait()
    tot_m = m_cross[0]
    for g in range(1, ngroup):
        tot_m = tot_m + m_cross[g]
    m_out[...] = jnp.full((8, ncol), jnp.sum(tot_m) / total_count, F32)


def hand_out(x, d, m, x_h, d_h, m_s, sem):
    copies = [pltpu.make_async_copy(x, x_h, sem.at[0]), pltpu.make_async_copy(d, d_h, sem.at[1])]
    for copy in copies:
        copy.start()
    m_s[0] = m[0, 0]
    for copy in copies:
        copy.wait()


def per_device(
    params, dual_in, jacobian, response, observed, psf, step_size, dual_step, tv_bound, clip_bound
):
    stokes, nwave, rows, ncol = observed.shape
    npar = params.shape[0]
    nimg = stokes * nwave
    images = stokes * npar
    width = -(-images // 8) * 8
    wide = -(-images // 16) * 16
    kdim = -(-3 * width // 128) * 128
    nrg = rows // HALO
    span = nrg + 2
    blk = HALO
    cols = ncol // blk
    unit = npar * blk
    edge = -(-unit // 16) * 16
    half_rows = 16 * -(-npar // 16)
    tiles = lax.axis_size("tile")
    waves = lax.axis_size("wave")
    total_count = float(nimg * waves * rows * tiles * ncol)
    gsize = group_size(tiles)
    ngroup = tiles // gsize
    vmem = pl.BlockSpec(memory_space=pltpu.VMEM)
    smem = pl.BlockSpec(memory_space=pltpu.SMEM)
    hbm = pl.BlockSpec(memory_space=pltpu.HBM)
    dma = pltpu.SemaphoreType.DMA
    state, dual_out, misfit = pl.pallas_call(
        functools.partial(kernel, tiles, waves, total_count),
        out_shape=(
            pltpu.VMEM((npar, rows, ncol), F32),
            pltpu.VMEM((2, npar, rows, ncol), F32),
            pltpu.VMEM((8, ncol), F32),
        ),
        in_specs=[hbm] * 4 + [vmem] * 2 + [smem] * 4,
        out_specs=(vmem, vmem, vmem),
        scratch_shapes=[
            pltpu.VMEM((npar, rows, ncol), F32),
            pltpu.VMEM((2, npar, rows, ncol), F32),
            pltpu.VMEM((images, rows, ncol), BF16),
            pltpu.VMEM((nimg, rows, ncol), BF16),
            pltpu.VMEM((span, nrg * ncol, 2 * ncol), BF16),
            pltpu.VMEM((TAPS * cols, ncol), F32),
            pltpu.VMEM((TAPS * cols, ncol), F32),
            pltpu.VMEM((nimg * rows, ncol), F32),
            pltpu.VMEM((blk * nimg, nrg * ncol), F32),
            pltpu.VMEM((width * rows, ncol), F32),
            pltpu.VMEM((span * blk * width, ncol), F32),
            pltpu.VMEM((span * blk * width, ncol), F32),
            pltpu.VMEM((span * blk * 2 * width, 2 * ncol), BF16),
            pltpu.VMEM((blk * 2 * width, nrg * ncol), F32),
            pltpu.VMEM((blk * wide, nrg * ncol), BF16),
            pltpu.VMEM((span * blk * width, ncol), F32),
            pltpu.VMEM((span * unit, ncol), F32),
            pltpu.VMEM((span * unit, ncol), F32),
            pltpu.VMEM((span * unit, ncol), F32),
            pltpu.VMEM((span * unit, ncol), F32),
            pltpu.VMEM((npar, rows, ncol), F32),
            pltpu.VMEM((npar, rows + 2 * HALO, ncol), F32),
            pltpu.VMEM((-(-npar // 8) * 8, nimg), F32),
            pltpu.VMEM((-(-TAPS // 8) * 8, ncol), F32),
            pltpu.VMEM((kdim, nimg), F32),
            pltpu.VMEM((nimg, kdim), BF16),
            pltpu.VMEM((2 * width, nimg), BF16),
            pltpu.VMEM((2, blk * width, ncol), BF16),
            pltpu.VMEM((blk * width, ncol), BF16),
            pltpu.VMEM((blk * width, ncol), BF16),
            pltpu.VMEM((2 * half_rows, ncol), F32),
            pltpu.VMEM((half_rows, ncol), F32),
            pltpu.VMEM((2 * half_rows, ncol), F32),
            pltpu.VMEM((half_rows, ncol), F32),
            pltpu.VMEM((span * unit, ncol), BF16),
            pltpu.VMEM((2, 2 * unit, ncol), BF16),
            pltpu.VMEM((nrg * unit, ncol), BF16),
            pltpu.VMEM((2, edge, ncol), BF16),
            pltpu.VMEM((waves, span * unit, ncol), BF16),
            pltpu.VMEM((waves, 2 * unit, ncol), BF16),
            pltpu.VMEM((waves, 2 * unit, ncol), BF16),
            pltpu.VMEM((waves, nrg * unit, ncol), BF16),
            pltpu.VMEM((waves, edge, ncol), BF16),
            pltpu.VMEM((waves, edge, ncol), BF16),
            pltpu.VMEM((8, ncol), F32),
            pltpu.VMEM((8, ncol), F32),
            pltpu.VMEM((gsize * waves, 8, ncol), F32),
            pltpu.VMEM((ngroup, 8, ncol), F32),
            dma((4,)),
            dma((8,)), dma((8,)),
            dma((2, waves)), dma((2, waves)),
            dma((2, waves)), dma((2, waves)),
            dma((2, waves)), dma((2, waves)),
            dma((gsize * waves,)), dma((gsize * waves,)),
            dma((ngroup,)), dma((ngroup,)),
        ],
        compiler_params=pltpu.CompilerParams(
            collective_id=0, has_side_effects=True, vmem_limit_bytes=66_000_000
        ),
    )(
        params, dual_in, jacobian.reshape(images, rows, ncol),
        observed.reshape(nimg, rows, ncol), response, psf,
        step_size.reshape(1), dual_step.reshape(1), tv_bound.reshape(1), clip_bound.reshape(1),
    )
    state, dual_out, misfit = pl.pallas_call(
        hand_out,
        out_shape=(
            jax.ShapeDtypeStruct((npar, rows, ncol), F32),
            jax.ShapeDtypeStruct((2, npar, rows, ncol), F32),
            jax.ShapeDtypeStruct((1,), F32),
        ),
        in_specs=[vmem] * 3,
        out_specs=(hbm, hbm, smem),
        scratch_shapes=[dma((2,))],
        compiler_params=pltpu.CompilerParams(vmem_limit_bytes=1_000_000),
    )(state, dual_out, misfit)
    return state, dual_out, misfit.reshape(())


def solution(mesh):
    in_specs = (
        P(None, "tile", None),
        P(None, None, "tile", None),
        P(None, None, "tile", None),
        P(None, "wave"),
        P(None, "wave", "tile", None),
        P(),
        P(),
        P(),
        P(),
        P(),
    )
    out_specs = (P(None, "tile", None), P(None, None, "tile", None), P())
    return jax.shard_map(
        per_device, mesh=mesh, in_specs=in_specs, out_specs=out_specs, check_vma=False
    )
```

time: 34 us -> 31.2 us (0.918)
  Pallas kernels: 30.5 us -> 27.7 us
    pallas_call x1, Pallas kernels: 29.3 us -> 26.5 us  [per_device(): pl.pallas_call(functools.partial(kernel, tiles, waves, total_count), out_...]
where the time goes in v2:
time: 31.2 us; the launch traced here: 30.9 us
  Pallas kernels  27.7 us (89%)
  between operations  3.22 us (10%)
    pallas_call x1, Pallas kernels, per_device(): pl.pallas_call(functools.partial(kernel, tiles, waves, total_count), out_...  26.5 us
    pallas_call x1, Pallas kernels, per_device(): pl.pallas_call(hand_out, out_shape=(jax.ShapeDtypeStruct((npar, rows, nco...  1.22 us

profile of v2, /device:TPU:0, one launch (start us, length us, event | category | flops | bytes accessed | tf_op | source)
XLA Modules:
  0.0 30.9 jit_solution(17115369966339270536)
XLA Ops:
  3.2 26.5 %shard_map.121 = (f32[9,16,128]{2,1,0:T(8,128)S(1)}, f32[2,9,16,128]{3,2,1,0:T(8,128)S(1)}, f32[8,128]{1,0:T(8,128)S(1)}) custom-call(f32[9,16,128]{2,1,0:T(8,128)} %params_h.1, f32[2,9,16,128]{3,2,1,0:T(8,128)} %dual_h.1, bf16[36,16,128]{2,1,0:T(8,128)(2,1)} %bitcast.12, bf16[128,16,128]{2,1,0:T(8,128)(2,1)} %bitcast.11, f32[9,32]{1,0:T(8,128)} %response.1, ...), custom_call_target="tpu_custom_call" | custom-call | tf_op jit(solution)/shard_map/pallas_call | solution.py:449
  29.7 1.2 %shard_map.122 = (f32[9,16,128]{2,1,0:T(8,128)}, f32[2,9,16,128]{3,2,1,0:T(8,128)}, f32[1]{0:T(128)}) custom-call(f32[9,16,128]{2,1,0:T(8,128)S(1)} %get-tuple-element.9.x, f32[2,9,16,128]{3,2,1,0:T(8,128)S(1)} %get-tuple-element.10.d, f32[8,128]{1,0:T(8,128)S(1)} %get-tuple-element.11.m), custom_call_target="tpu_custom_call" | custom-call | tf_op jit(solution)/shard_map/pallas_call | solution.py:523

commit v3 on v2

--- a/solution.py
+++ b/solution.py
@@ -28,12 +28,12 @@
 
 def kernel(
     tiles, waves, total_count,
-    params_h, dual_h, jac_h, obs_h, response, psf, step_size, dual_step, tv_bound, clip_bound,
+    params_h, dual_h, jac_h, obs_h, response_h, psf_h, step_h, dstep_h, bound_h, clip_h,
     x_out, d_out, m_out,
-    params, dual, jac, obs,
+    response, psf, step_size, dual_step, tv_bound, clip_bound, params, dual, jac, obs,
     wt, main_a, half_a, obs_f, obs_l, jac_n, jac_l, x_l, lhs, tot, proj, prod, grad_c,
     x_c, div_c, base_c, div_n, dpad, respad, psfpad, rt, rbf, rtb,
-    jac_edge, jac_up, jac_dn, row_dn, row_up, row_above, row_below,
+    jac_up, jac_dn, par_up, par_dn, dual_up, jac_hn,
     full0, edge0, full1, edge1, full0_in, up0_in, dn0_in, full1_in, up1_in, dn1_in,
     m_own, m_mid, m_group, m_cross,
     local, in_send, in_recv, f_send, f_recv, u_send, u_recv, d_send, d_recv,
@@ -51,7 +51,6 @@
     blk = HALO
     cols = ncol // blk
     unit = npar * blk
-    half_rows = 16 * -(-npar // 16)
     me_t = lax.axis_index("tile")
     me_w = lax.axis_index("wave")
     up = lax.rem(me_t + tiles - 1, tiles)
@@ -77,6 +76,12 @@
         pltpu.make_async_copy(params_h, params, local.at[1]),
         pltpu.make_async_copy(dual_h, dual, local.at[2]),
         pltpu.make_async_copy(obs_h, obs, local.at[3]),
+        pltpu.make_async_copy(psf_h, psf, local.at[4]),
+        pltpu.make_async_copy(response_h, response, local.at[5]),
+        pltpu.make_async_copy(step_h, step_size, local.at[6]),
+        pltpu.make_async_copy(dstep_h, dual_step, local.at[7]),
+        pltpu.make_async_copy(bound_h, tv_bound, local.at[8]),
+        pltpu.make_async_copy(clip_h, clip_bound, local.at[9]),
     ]
     for copy in fetch:
         copy.start()
@@ -104,35 +109,18 @@
     def unit_rows(rg, b):
         return slice((rg * blk + b) * npar, (rg * blk + b + 1) * npar)
 
-    def to_units(source, target, rg_from, rg_to):
+    def to_units(source, rg_from, target, rg_to):
         parts = swap_blocks([source[:, rg_from * HALO + r, :] for r in range(HALO)])
         for b in range(blk):
             target[unit_rows(rg_to, b), :] = parts[b]
 
-    jac_n[images * rows:, :] = jnp.zeros((jac_n.shape[0] - images * rows, ncol), F32)
-    fetch[0].wait()
-    for m in range(images):
-        jac_n[m * rows:(m + 1) * rows, :] = jac[m].astype(F32)
-    for rg in range(nrg):
+    def to_blocks(source, height, rg_from, rg_to):
         for g in range(width // 8):
-            parts = swap_blocks(
-                [jac_n[pl.ds(g * 8 * rows + rg * HALO + r, 8, stride=rows), :] for r in range(HALO)]
-            )
+            at = g * 8 * height + rg_from * HALO
+            parts = swap_blocks([source[pl.ds(at + r, 8, stride=height), :] for r in range(HALO)])
             for b in range(blk):
-                at = ((rg + 1) * blk + b) * width + g * 8
+                at = (rg_to * blk + b) * width + g * 8
                 jac_l[at:at + 8, :] = parts[b]
-    jac_edge[0] = jac_l[blk * width:2 * blk * width, :].astype(BF16)
-    jac_edge[1] = jac_l[nrg * blk * width:(nrg + 1) * blk * width, :].astype(BF16)
-    fetch[1].wait()
-    for rg in range(nrg):
-        to_units(params, x_c, rg, rg + 1)
-    fetch[2].wait()
-    row_dn[...] = jnp.zeros_like(row_dn)
-    row_up[...] = jnp.zeros_like(row_up)
-    row_dn[0:npar, :] = params[:, rows - 1, :]
-    row_dn[half_rows:half_rows + npar, :] = dual[0, :, rows - 1, :]
-    row_up[0:npar, :] = params[:, 0, :]
-    pl.semaphore_wait(barrier, len(peers))
 
     def remote(src, dst, send, recv, peer):
         return pltpu.make_async_remote_copy(
@@ -145,22 +133,15 @@
     def unit_span(rg, count):
         return pl.ds(rg * unit, count * unit)
 
+    top, last = pl.ds(0, HALO), pl.ds(rows - HALO, HALO)
     first = [
-        remote(row_dn, row_above, in_send.at[0], in_recv.at[0], below),
-        remote(row_up, row_below, in_send.at[1], in_recv.at[1], above),
-        remote(jac_edge.at[1], jac_up, in_send.at[2], in_recv.at[2], below),
-        remote(jac_edge.at[0], jac_dn, in_send.at[3], in_recv.at[3], above),
-        remote(x_c.at[unit_span(nrg, 1)], x_c.at[unit_span(0, 1)], in_send.at[4], in_recv.at[4], below),
-        remote(x_c.at[unit_span(1, 1)], x_c.at[unit_span(nrg + 1, 1)], in_send.at[5], in_recv.at[5], above),
+        remote(jac_h.at[:, last], jac_up, in_send.at[0], in_recv.at[0], below),
+        remote(jac_h.at[:, top], jac_dn, in_send.at[1], in_recv.at[1], above),
+        remote(params_h.at[:, last], par_up, in_send.at[2], in_recv.at[2], below),
+        remote(params_h.at[:, top], par_dn, in_send.at[3], in_recv.at[3], above),
+        remote(dual_h.at[0, :, last], dual_up, in_send.at[4], in_recv.at[4], below),
     ]
-    for copy in first:
-        copy.start()
-
-    step = step_size[0]
-    clip = clip_bound[0]
-    bound = tv_bound[0]
-    dstep = dual_step[0]
-
+    fetch[4].wait()
     psfpad[...] = jnp.zeros_like(psfpad)
     psfpad[0:TAPS, 0:TAPS] = psf[...].astype(F32)
     taps = pltpu.roll(psfpad[...], ncol - HALO, 1)
@@ -173,7 +154,6 @@
             for b in range(3):
                 value = value + pltpu.roll(value, cols << b, 1)
             ref[tap * cols:(tap + 1) * cols, :] = value
-    edge1[...] = jnp.zeros_like(edge1)
     wt[0, ncol:, :] = jnp.zeros((wt.shape[1] - ncol, 2 * ncol), BF16)
     for rg in range(1, span):
         for ro in range(nrg):
@@ -192,6 +172,29 @@
                     at = ro * ncol + r * cols
                     wt[ro + delta, at:at + cols, part * ncol:(part + 1) * ncol] = value
 
+    pl.semaphore_wait(barrier, len(peers))
+    for copy in first:
+        copy.start()
+
+    jac_n[images * rows:, :] = jnp.zeros((jac_n.shape[0] - images * rows, ncol), F32)
+    jac_hn[images * HALO:, :] = jnp.zeros((jac_hn.shape[0] - images * HALO, ncol), F32)
+    edge1[...] = jnp.zeros_like(edge1)
+    fetch[0].wait()
+    for m in range(images):
+        jac_n[m * rows:(m + 1) * rows, :] = jac[m].astype(F32)
+    for rg in range(nrg):
+        to_blocks(jac_n, rows, rg, rg + 1)
+    fetch[1].wait()
+    for rg in range(nrg):
+        to_units(params, rg, x_c, rg + 1)
+    for copy in fetch[5:]:
+        copy.wait()
+
+    step = step_size[0]
+    clip = clip_bound[0]
+    bound = tv_bound[0]
+    dstep = dual_step[0]
+
     def expand(rg):
         for b in range(blk):
             value = x_c[unit_rows(rg, b), :]
@@ -243,46 +246,26 @@
     rbf[...] = jnp.where(place < 2 * width, high, low).T.astype(BF16)
     rtb[...] = jnp.concatenate([high[0:width], low[0:width]], axis=0).astype(BF16)
 
-    d1 = params[...]
-    d1 = pltpu.roll(d1, ncol - 1, 2) - d1
-    d1 = jnp.clip(dual[1] + dstep * d1, -bound, bound)
-    d_out[1] = d1
     fetch[3].wait()
     obs_f[...] = obs[...].astype(F32).reshape(nimg * rows, ncol)
-    for g in range(nimg // 8):
+    def turn(g, carry):
         for rg in range(nrg):
-            parts = swap_blocks(
-                [obs_f[pl.ds(g * 8 * rows + rg * HALO + r, 8, stride=rows), :] for r in range(HALO)]
-            )
+            source = pl.multiple_of(g * 8 * rows, 8 * rows) + rg * HALO
+            parts = swap_blocks([obs_f[pl.ds(source + r, 8, stride=rows), :] for r in range(HALO)])
             for b in range(blk):
-                at = b * nimg + g * 8
-                obs_l[at:at + 8, rg * ncol:(rg + 1) * ncol] = parts[b]
-
-    for copy in first[:2]:
+                at = pl.multiple_of(b * nimg + g * 8, 8)
+                obs_l[pl.ds(at, 8), rg * ncol:(rg + 1) * ncol] = parts[b]
+        return carry
+
+    lax.fori_loop(0, nimg // 8, turn, 0, unroll=4)
+    for copy in first[:4]:
         copy.wait()
-    now = params[...]
-    dpad[:, HALO:HALO + rows, :] = now
-    dpad[:, HALO + rows, :] = row_below[0:npar, :]
-    d0 = dpad[:, HALO + 1:HALO + 1 + rows, :] - now
-    d0 = jnp.clip(dual[0] + dstep * d0, -bound, bound)
-    d_out[0] = d0
-    side = params[:, 0, :] - row_above[0:npar, :]
-    side = jnp.clip(row_above[half_rows:half_rows + npar, :] + dstep * side, -bound, bound)
-    dpad[:, HALO - 1, :] = side
-    dpad[:, HALO:HALO + rows, :] = d0
-    div_n[...] = (d0 - dpad[:, HALO - 1:HALO - 1 + rows, :]) + (d1 - pltpu.roll(d1, 1, 2))
-    for rg in range(nrg):
-        to_units(div_n, div_c, rg, rg + 1)
-    copies_v = [
-        remote(div_c.at[unit_span(nrg, 1)], div_c.at[unit_span(0, 1)], in_send.at[6], in_recv.at[6], below),
-        remote(div_c.at[unit_span(1, 1)], div_c.at[unit_span(nrg + 1, 1)], in_send.at[7], in_recv.at[7], above),
-    ]
-    for copy in copies_v:
-        copy.start()
-    for copy in first[2:]:
-        copy.wait()
-    jac_l[0:blk * width, :] = jac_up[...].astype(F32)
-    jac_l[(nrg + 1) * blk * width:, :] = jac_dn[...].astype(F32)
+    for source, rg in ((jac_up, 0), (jac_dn, nrg + 1)):
+        for m in range(images):
+            jac_hn[m * HALO:(m + 1) * HALO, :] = source[m].astype(F32)
+        to_blocks(jac_hn, HALO, 0, rg)
+    to_units(par_up, 0, x_c, 0)
+    to_units(par_dn, 0, x_c, nrg + 1)
     zero_k = jnp.zeros((rbf.shape[1] - 3 * width, nrg * ncol), F32)
 
     def widen(value):
@@ -303,11 +286,17 @@
                 part = forward(rg)
                 total = part if total is None else total + part
         loss = jnp.zeros((8, nrg * ncol), F32)
-        for b in range(blk):
+        def respond(b):
             both = total[b * 2 * width:(b + 1) * 2 * width]
             bhi, blo = split_hi_lo(both[:width] + both[width:])
             stack = jnp.concatenate([bhi, blo, bhi, zero_k], axis=0).astype(BF16)
-            blurred = jnp.dot(rbf[...], stack, preferred_element_type=F32)
+            return jnp.dot(rbf[...], stack, preferred_element_type=F32)
+
+        coming = respond(0)
+        for b in range(blk):
+            blurred = coming
+            if b + 1 < blk:
+                coming = respond(b + 1)
             resid = blurred - obs_l[b * nimg:(b + 1) * nimg, :]
             held = jnp.clip(resid, -clip, clip)
             if it == 0:
@@ -362,6 +351,36 @@
         for copy in copies:
             copy.start()
         if it == 0:
+            fetch[2].wait()
+            first[4].wait()
+            now = params[...]
+            d1 = pltpu.roll(now, ncol - 1, 2) - now
+            d1 = jnp.clip(dual[1] + dstep * d1, -bound, bound)
+            d_out[1] = d1
+            dpad[:, HALO:HALO + rows, :] = now
+            dpad[:, HALO + rows, :] = par_dn[:, 0, :]
+            d0 = dpad[:, HALO + 1:HALO + 1 + rows, :] - now
+            d0 = jnp.clip(dual[0] + dstep * d0, -bound, bound)
+            d_out[0] = d0
+            side = params[:, 0, :] - par_up[:, HALO - 1, :]
+            side = jnp.clip(dual_up[:, HALO - 1, :] + dstep * side, -bound, bound)
+            dpad[:, HALO - 1, :] = side
+            dpad[:, HALO:HALO + rows, :] = d0
+            div_n[...] = (d0 - dpad[:, HALO - 1:HALO - 1 + rows, :]) + (d1 - pltpu.roll(d1, 1, 2))
+            for rg in range(nrg):
+                to_units(div_n, rg, div_c, rg + 1)
+            copies_v = [
+                remote(
+                    div_c.at[unit_span(nrg, 1)], div_c.at[unit_span(0, 1)],
+                    in_send.at[5], in_recv.at[5], below,
+                ),
+                remote(
+                    div_c.at[unit_span(1, 1)], div_c.at[unit_span(nrg + 1, 1)],
+                    in_send.at[6], in_recv.at[6], above,
+                ),
+            ]
+            for copy in copies_v:
+                copy.start()
             for copy in copies_v:
                 copy.wait()
             base_c[...] = x_c[...] + step * div_c[...]
@@ -380,6 +399,12 @@
             ]
             for copy in copies_c:
                 copy.start()
+            for copy in copies_c:
+                copy.wait()
+            tot_m = m_cross[0]
+            for g in range(1, ngroup):
+                tot_m = tot_m + m_cross[g]
+            m_out[...] = jnp.full((8, ncol), jnp.sum(tot_m) / total_count, F32)
         for copy in copies:
             copy.wait()
 
@@ -403,19 +428,15 @@
         parts = swap_blocks([x_c[unit_rows(rg + 1, b), :] for b in range(blk)])
         for r in range(HALO):
             x_out[:, rg * HALO + r, :] = parts[r]
-    for copy in copies_c:
-        copy.wait()
-    tot_m = m_cross[0]
-    for g in range(1, ngroup):
-        tot_m = tot_m + m_cross[g]
-    m_out[...] = jnp.full((8, ncol), jnp.sum(tot_m) / total_count, F32)
-
-
-def hand_out(x, d, m, x_h, d_h, m_s, sem):
+
+
+def hand_out(x, d, m, x_h, d_h, m_h, m_s, sem):
     copies = [pltpu.make_async_copy(x, x_h, sem.at[0]), pltpu.make_async_copy(d, d_h, sem.at[1])]
     for copy in copies:
         copy.start()
     m_s[0] = m[0, 0]
+    copies.append(pltpu.make_async_copy(m_s, m_h, sem.at[2]))
+    copies[2].start()
     for copy in copies:
         copy.wait()
 
@@ -436,7 +457,6 @@
     cols = ncol // blk
     unit = npar * blk
     edge = -(-unit // 16) * 16
-    half_rows = 16 * -(-npar // 16)
     tiles = lax.axis_size("tile")
     waves = lax.axis_size("wave")
     total_count = float(nimg * waves * rows * tiles * ncol)
@@ -453,9 +473,15 @@
             pltpu.VMEM((2, npar, rows, ncol), F32),
             pltpu.VMEM((8, ncol), F32),
         ),
-        in_specs=[hbm] * 4 + [vmem] * 2 + [smem] * 4,
+        in_specs=[hbm] * 10,
         out_specs=(vmem, vmem, vmem),
         scratch_shapes=[
+            pltpu.VMEM(response.shape, F32),
+            pltpu.VMEM(psf.shape, BF16),
+            pltpu.SMEM((1,), F32),
+            pltpu.SMEM((1,), F32),
+            pltpu.SMEM((1,), F32),
+            pltpu.SMEM((1,), F32),
             pltpu.VMEM((npar, rows, ncol), F32),
             pltpu.VMEM((2, npar, rows, ncol), F32),
             pltpu.VMEM((images, rows, ncol), BF16),
@@ -483,13 +509,12 @@
             pltpu.VMEM((kdim, nimg), F32),
             pltpu.VMEM((nimg, kdim), BF16),
             pltpu.VMEM((2 * width, nimg), BF16),
-            pltpu.VMEM((2, blk * width, ncol), BF16),
-            pltpu.VMEM((blk * width, ncol), BF16),
-            pltpu.VMEM((blk * width, ncol), BF16),
-            pltpu.VMEM((2 * half_rows, ncol), F32),
-            pltpu.VMEM((half_rows, ncol), F32),
-            pltpu.VMEM((2 * half_rows, ncol), F32),
-            pltpu.VMEM((half_rows, ncol), F32),
+            pltpu.VMEM((images, HALO, ncol), BF16),
+            pltpu.VMEM((images, HALO, ncol), BF16),
+            pltpu.VMEM((npar, HALO, ncol), F32),
+            pltpu.VMEM((npar, HALO, ncol), F32),
+            pltpu.VMEM((npar, HALO, ncol), F32),
+            pltpu.VMEM((width * HALO, ncol), F32),
             pltpu.VMEM((span * unit, ncol), BF16),
             pltpu.VMEM((2, 2 * unit, ncol), BF16),
             pltpu.VMEM((nrg * unit, ncol), BF16),
@@ -504,8 +529,8 @@
             pltpu.VMEM((8, ncol), F32),
             pltpu.VMEM((gsize * waves, 8, ncol), F32),
             pltpu.VMEM((ngroup, 8, ncol), F32),
-            dma((4,)),
-            dma((8,)), dma((8,)),
+            dma((10,)),
+            dma((7,)), dma((7,)),
             dma((2, waves)), dma((2, waves)),
             dma((2, waves)), dma((2, waves)),
             dma((2, waves)), dma((2, waves)),
@@ -528,8 +553,8 @@
             jax.ShapeDtypeStruct((1,), F32),
         ),
         in_specs=[vmem] * 3,
-        out_specs=(hbm, hbm, smem),
-        scratch_shapes=[dma((2,))],
+        out_specs=(hbm, hbm, hbm),
+        scratch_shapes=[pltpu.SMEM((1,), F32), dma((3,))],
         compiler_params=pltpu.CompilerParams(vmem_limit_bytes=1_000_000),
     )(state, dual_out, misfit)
     return state, dual_out, misfit.reshape(())

time: 31.2 us -> 28.4 us (0.910)
  Pallas kernels: 27.7 us -> 25 us
    pallas_call x1, Pallas kernels: 26.5 us -> 24.3 us  [per_device(): pl.pallas_call(functools.partial(kernel, tiles, waves, total_count), out_...]
    pallas_call x1, Pallas kernels: 1.22 us -> 0.72 us  [per_device(): pl.pallas_call(hand_out, out_shape=(jax.ShapeDtypeStruct((npar, rows, nco...]
where the time goes in v3:
time: 28.4 us; the launch traced here: 28.2 us
  Pallas kernels  25 us (88%)
  between operations  3.22 us (11%)
    pallas_call x1, Pallas kernels, per_device(): pl.pallas_call(functools.partial(kernel, tiles, waves, total_count), out_...  24.3 us
    pallas_call x1, Pallas kernels, per_device(): pl.pallas_call(hand_out, out_shape=(jax.ShapeDtypeStruct((npar, rows, nco...  0.72 us

profile of v3, /device:TPU:0, one launch (start us, length us, event | category | flops | bytes accessed | tf_op | source)
XLA Modules:
  0.0 28.2 jit_solution(16909516804899168302)
XLA Ops:
  3.2 24.3 %shard_map.121 = (f32[9,16,128]{2,1,0:T(8,128)S(1)}, f32[2,9,16,128]{3,2,1,0:T(8,128)S(1)}, f32[8,128]{1,0:T(8,128)S(1)}) custom-call(f32[9,16,128]{2,1,0:T(8,128)} %params_h.1, f32[2,9,16,128]{3,2,1,0:T(8,128)} %dual_h.1, bf16[36,16,128]{2,1,0:T(8,128)(2,1)} %bitcast.12, bf16[128,16,128]{2,1,0:T(8,128)(2,1)} %bitcast.11, f32[9,32]{1,0:T(8,128)} %response_h.1, ...), custom_call_target="tpu_custom_call" | custom-call | tf_op jit(solution)/shard_map/pallas_call | solution.py:469
  27.5 0.7 %shard_map.122 = (f32[9,16,128]{2,1,0:T(8,128)}, f32[2,9,16,128]{3,2,1,0:T(8,128)}, f32[1]{0:T(128)}) custom-call(f32[9,16,128]{2,1,0:T(8,128)S(1)} %get-tuple-element.9.x, f32[2,9,16,128]{3,2,1,0:T(8,128)S(1)} %get-tuple-element.10.d, f32[8,128]{1,0:T(8,128)S(1)} %get-tuple-element.11.m), custom_call_target="tpu_custom_call" | custom-call | tf_op jit(solution)/shard_map/pallas_call | solution.py:548

commit v4 on v3

--- a/solution.py
+++ b/solution.py
@@ -45,7 +45,6 @@
     nwave = response.shape[1]
     nimg = stokes * nwave
     width = -(-images // 8) * 8
-    wide = -(-images // 16) * 16
     nrg = rows // HALO
     span = nrg + 2
     blk = HALO
@@ -268,12 +267,6 @@
     to_units(par_dn, 0, x_c, nrg + 1)
     zero_k = jnp.zeros((rbf.shape[1] - 3 * width, nrg * ncol), F32)
 
-    def widen(value):
-        if wide == width:
-            return value.astype(BF16)
-        fill = jnp.zeros((wide - width, value.shape[1]), F32)
-        return jnp.concatenate([value, fill], axis=0).astype(BF16)
-
     for it in range(2):
         for rg in (0, nrg + 1) if it == 0 else range(span):
             expand(rg)
@@ -292,18 +285,29 @@
             stack = jnp.concatenate([bhi, blo, bhi, zero_k], axis=0).astype(BF16)
             return jnp.dot(rbf[...], stack, preferred_element_type=F32)
 
-        coming = respond(0)
+        def collect(b, held, before):
+            both = jnp.dot(rtb[...], held, preferred_element_type=F32)
+            both = both[:width] + both[width:]
+            if b % 2 == 1:
+                pair = jnp.concatenate([before, both], axis=0).astype(BF16)
+                proj[(b - 1) * width:(b + 1) * width, :] = pair
+            return both
+
+        ahead = [respond(b) for b in range(4)]
+        held_last = before = None
         for b in range(blk):
-            blurred = coming
-            if b + 1 < blk:
-                coming = respond(b + 1)
+            if b + 4 < blk:
+                ahead.append(respond(b + 4))
+            blurred = ahead.pop(0)
             resid = blurred - obs_l[b * nimg:(b + 1) * nimg, :]
             held = jnp.clip(resid, -clip, clip)
             if it == 0:
                 huber = held * (resid - 0.5 * held)
                 loss = loss + jnp.sum(huber.reshape(nimg // 8, 8, nrg * ncol), axis=0)
-            both = jnp.dot(rtb[...], held.astype(BF16), preferred_element_type=F32)
-            proj[b * wide:(b + 1) * wide, :] = widen(both[:width] + both[width:])
+            if b > 0:
+                before = collect(b - 1, held_last, before)
+            held_last = held.astype(BF16)
+        collect(blk - 1, held_last, before)
         if it == 0:
             loss = sum(loss[:, i * ncol:(i + 1) * ncol] for i in range(nrg))
             m_own[...] = loss
@@ -316,9 +320,10 @@
             for copy in copies_g:
                 copy.start()
         for rg in range(span):
-            back = jnp.dot(proj[...], wt[rg], preferred_element_type=F32)
-            mains = [back[b * wide:b * wide + width, 0:ncol] for b in range(blk)]
-            sides = [back[b * wide:b * wide + width, ncol:] for b in range(blk)]
+            used = slice(max(rg - 2, 0) * ncol, min(rg + 1, nrg) * ncol)
+            back = jnp.dot(proj[:, used], wt[rg, used, :], preferred_element_type=F32)
+            mains = [back[b * width:(b + 1) * width, 0:ncol] for b in range(blk)]
+            sides = [back[b * width:(b + 1) * width, ncol:] for b in range(blk)]
             for b in range(blk):
                 along = mains[b] + jnp.where(near, sides[(b + blk - 1) % blk], sides[(b + 1) % blk])
                 at = (rg * blk + b) * width
@@ -449,7 +454,6 @@
     nimg = stokes * nwave
     images = stokes * npar
     width = -(-images // 8) * 8
-    wide = -(-images // 16) * 16
     kdim = -(-3 * width // 128) * 128
     nrg = rows // HALO
     span = nrg + 2
@@ -496,7 +500,7 @@
             pltpu.VMEM((span * blk * width, ncol), F32),
             pltpu.VMEM((span * blk * 2 * width, 2 * ncol), BF16),
             pltpu.VMEM((blk * 2 * width, nrg * ncol), F32),
-            pltpu.VMEM((blk * wide, nrg * ncol), BF16),
+            pltpu.VMEM((blk * width, nrg * ncol), BF16),
             pltpu.VMEM((span * blk * width, ncol), F32),
             pltpu.VMEM((span * unit, ncol), F32),
             pltpu.VMEM((span * unit, ncol), F32),

time: 28.4 us -> 27.9 us (0.982)
  Pallas kernels: 25 us -> 24.5 us
    pallas_call x1, Pallas kernels: 24.3 us -> 23.8 us  [per_device(): pl.pallas_call(functools.partial(kernel, tiles, waves, total_count), out_...]
where the time goes in v4:
time: 27.9 us; the launch traced here: 27.7 us
  Pallas kernels  24.5 us (88%)
  between operations  3.22 us (12%)
    pallas_call x1, Pallas kernels, per_device(): pl.pallas_call(functools.partial(kernel, tiles, waves, total_count), out_...  23.8 us
    pallas_call x1, Pallas kernels, per_device(): pl.pallas_call(hand_out, out_shape=(jax.ShapeDtypeStruct((npar, rows, nco...  0.72 us

profile of v4, /device:TPU:0, one launch (start us, length us, event | category | flops | bytes accessed | tf_op | source)
XLA Modules:
  0.0 27.7 jit_solution(17247603470419767622)
XLA Ops:
  3.2 23.8 %shard_map.121 = (f32[9,16,128]{2,1,0:T(8,128)S(1)}, f32[2,9,16,128]{3,2,1,0:T(8,128)S(1)}, f32[8,128]{1,0:T(8,128)S(1)}) custom-call(f32[9,16,128]{2,1,0:T(8,128)} %params_h.1, f32[2,9,16,128]{3,2,1,0:T(8,128)} %dual_h.1, bf16[36,16,128]{2,1,0:T(8,128)(2,1)} %bitcast.12, bf16[128,16,128]{2,1,0:T(8,128)(2,1)} %bitcast.11, f32[9,32]{1,0:T(8,128)} %response_h.1, ...), custom_call_target="tpu_custom_call" | custom-call | tf_op jit(solution)/shard_map/pallas_call | solution.py:473
  27.0 0.7 %shard_map.122 = (f32[9,16,128]{2,1,0:T(8,128)}, f32[2,9,16,128]{3,2,1,0:T(8,128)}, f32[1]{0:T(128)}) custom-call(f32[9,16,128]{2,1,0:T(8,128)S(1)} %get-tuple-element.9.x, f32[2,9,16,128]{3,2,1,0:T(8,128)S(1)} %get-tuple-element.10.d, f32[8,128]{1,0:T(8,128)S(1)} %get-tuple-element.11.m), custom_call_target="tpu_custom_call" | custom-call | tf_op jit(solution)/shard_map/pallas_call | solution.py:552

commit v5 on v4

--- a/solution.py
+++ b/solution.py
@@ -36,8 +36,8 @@
     jac_up, jac_dn, par_up, par_dn, dual_up, jac_hn,
     full0, edge0, full1, edge1, full0_in, up0_in, dn0_in, full1_in, up1_in, dn1_in,
     m_own, m_mid, m_group, m_cross,
-    local, in_send, in_recv, f_send, f_recv, u_send, u_recv, d_send, d_recv,
-    mg_send, mg_recv, mc_send, mc_recv,
+    local, in_send, in_recv, f_recv, u_recv, d_recv,
+    mg_send, mg_recv, mc_recv,
 ):
     npar, rows, ncol = params.shape
     images = jac.shape[0]
@@ -186,6 +186,7 @@
     fetch[1].wait()
     for rg in range(nrg):
         to_units(params, rg, x_c, rg + 1)
+    fetch[2].wait()
     for copy in fetch[5:]:
         copy.wait()
 
@@ -257,12 +258,14 @@
         return carry
 
     lax.fori_loop(0, nimg // 8, turn, 0, unroll=4)
-    for copy in first[:4]:
+    for copy in first[:2]:
         copy.wait()
     for source, rg in ((jac_up, 0), (jac_dn, nrg + 1)):
         for m in range(images):
             jac_hn[m * HALO:(m + 1) * HALO, :] = source[m].astype(F32)
         to_blocks(jac_hn, HALO, 0, rg)
+    for copy in first[2:4]:
+        copy.wait()
     to_units(par_up, 0, x_c, 0)
     to_units(par_dn, 0, x_c, nrg + 1)
     zero_k = jnp.zeros((rbf.shape[1] - 3 * width, nrg * ncol), F32)
@@ -310,16 +313,8 @@
         collect(blk - 1, held_last, before)
         if it == 0:
             loss = sum(loss[:, i * ncol:(i + 1) * ncol] for i in range(nrg))
-            m_own[...] = loss
-            slot = my_place * waves + me_w
-            m_group[slot] = loss
-            copies_g = [
-                remote(m_own, m_group.at[slot], mg_send.at[d], mg_recv.at[d], peer)
-                for d, peer in enumerate(group_peers)
-            ]
-            for copy in copies_g:
-                copy.start()
-        for rg in range(span):
+
+        def backward(rg):
             used = slice(max(rg - 2, 0) * ncol, min(rg + 1, nrg) * ncol)
             back = jnp.dot(proj[:, used], wt[rg, used, :], preferred_element_type=F32)
             mains = [back[b * width:(b + 1) * width, 0:ncol] for b in range(blk)]
@@ -338,25 +333,46 @@
         start = 0 if it == 0 else unit
         full_out, edge_out = (full0, edge0) if it == 0 else (full1, edge1)
         full_in, up_in, dn_in = (full0_in, up0_in, dn0_in) if it == 0 else (full1_in, up1_in, dn1_in)
-        edge_out[0, 0:reach, :] = grad_c[0:reach, :].astype(BF16)
-        edge_out[1, 0:reach, :] = grad_c[size - reach:, :].astype(BF16)
+        copies = []
+
+        def send_edges():
+            edge_out[0, 0:reach, :] = grad_c[0:reach, :].astype(BF16)
+            edge_out[1, 0:reach, :] = grad_c[size - reach:, :].astype(BF16)
+            for d in range(waves - 1, -1, -1):
+                copies.append(remote(
+                    edge_out.at[1], up_in.at[me_w], local.at[d], u_recv.at[it, d], (down, spin[d])
+                ))
+                copies.append(remote(
+                    edge_out.at[0], dn_in.at[me_w], local.at[waves + d], d_recv.at[it, d], (up, spin[d])
+                ))
+            for copy in copies:
+                copy.start()
+
+        backward(0)
+        backward(nrg + 1)
+        if it == 1:
+            send_edges()
+        for rg in range(1, nrg + 1):
+            backward(rg)
+        if it == 0:
+            send_edges()
         whole = grad_c[start:size - start, :].astype(BF16)
         full_out[...] = whole
         full_in[me_w] = whole
-        copies = []
-        for d in range(waves - 1, -1, -1):
-            copies += [
-                remote(edge_out.at[1], up_in.at[me_w], u_send.at[it, d], u_recv.at[it, d], (down, spin[d])),
-                remote(edge_out.at[0], dn_in.at[me_w], d_send.at[it, d], d_recv.at[it, d], (up, spin[d])),
+        for d in range(1, waves):
+            copy = remote(full_out, full_in.at[me_w], local.at[2 * waves + d - 1], f_recv.at[it, d - 1], (me_t, spin[d]))
+            copy.start()
+            copies.append(copy)
+        if it == 0:
+            m_own[...] = loss
+            slot = my_place * waves + me_w
+            m_group[slot] = loss
+            copies_g = [
+                remote(m_own, m_group.at[slot], mg_send.at[d], mg_recv.at[d], peer)
+                for d, peer in enumerate(group_peers)
             ]
-        for d in range(1, waves):
-            copies.append(
-                remote(full_out, full_in.at[me_w], f_send.at[it, d], f_recv.at[it, d], (me_t, spin[d]))
-            )
-        for copy in copies:
-            copy.start()
-        if it == 0:
-            fetch[2].wait()
+            for copy in copies_g:
+                copy.start()
             first[4].wait()
             now = params[...]
             d1 = pltpu.roll(now, ncol - 1, 2) - now
@@ -399,7 +415,7 @@
             m_mid[...] = total_m
             m_cross[my_group] = total_m
             copies_c = [
-                remote(m_mid, m_cross.at[my_group], mc_send.at[d], mc_recv.at[d], peer)
+                remote(m_mid, m_cross.at[my_group], in_send.at[d], mc_recv.at[d], peer)
                 for d, peer in enumerate(cross_peers)
             ]
             for copy in copies_c:
@@ -533,13 +549,13 @@
             pltpu.VMEM((8, ncol), F32),
             pltpu.VMEM((gsize * waves, 8, ncol), F32),
             pltpu.VMEM((ngroup, 8, ncol), F32),
-            dma((10,)),
-            dma((7,)), dma((7,)),
-            dma((2, waves)), dma((2, waves)),
-            dma((2, waves)), dma((2, waves)),
-            dma((2, waves)), dma((2, waves)),
-            dma((gsize * waves,)), dma((gsize * waves,)),
-            dma((ngroup,)), dma((ngroup,)),
+            dma((max(10, 3 * waves - 1),)),
+            dma((max(7, ngroup - 1),)), dma((7,)),
+            dma((2, max(1, waves - 1))),
+            dma((2, waves)),
+            dma((2, waves)),
+            dma((max(1, gsize * waves - 1),)), dma((max(1, gsize * waves - 1),)),
+            dma((max(1, ngroup - 1),)),
         ],
         compiler_params=pltpu.CompilerParams(
             collective_id=0, has_side_effects=True, vmem_limit_bytes=66_000_000

time: 27.9 us -> 27.6 us (0.989)
  no operation moved by 1% of the time
where the time goes in v5:
time: 27.6 us; the launch traced here: 27.5 us
  Pallas kernels  24.3 us (88%)
  between operations  3.22 us (12%)
    pallas_call x1, Pallas kernels, per_device(): pl.pallas_call(functools.partial(kernel, tiles, waves, total_count), out_...  23.5 us
    pallas_call x1, Pallas kernels, per_device(): pl.pallas_call(hand_out, out_shape=(jax.ShapeDtypeStruct((npar, rows, nco...  0.72 us

profile of v5, /device:TPU:0, one launch (start us, length us, event | category | flops | bytes accessed | tf_op | source)
XLA Modules:
  0.0 27.5 jit_solution(12080989683982401669)
XLA Ops:
  3.2 23.5 %shard_map.121 = (f32[9,16,128]{2,1,0:T(8,128)S(1)}, f32[2,9,16,128]{3,2,1,0:T(8,128)S(1)}, f32[8,128]{1,0:T(8,128)S(1)}) custom-call(f32[9,16,128]{2,1,0:T(8,128)} %params_h.1, f32[2,9,16,128]{3,2,1,0:T(8,128)} %dual_h.1, bf16[36,16,128]{2,1,0:T(8,128)(2,1)} %bitcast.12, bf16[128,16,128]{2,1,0:T(8,128)(2,1)} %bitcast.11, f32[9,32]{1,0:T(8,128)} %response_h.1, ...), custom_call_target="tpu_custom_call" | custom-call | tf_op jit(solution)/shard_map/pallas_call | solution.py:489
  26.8 0.7 %shard_map.122 = (f32[9,16,128]{2,1,0:T(8,128)}, f32[2,9,16,128]{3,2,1,0:T(8,128)}, f32[1]{0:T(128)}) custom-call(f32[9,16,128]{2,1,0:T(8,128)S(1)} %get-tuple-element.9.x, f32[2,9,16,128]{3,2,1,0:T(8,128)S(1)} %get-tuple-element.10.d, f32[8,128]{1,0:T(8,128)S(1)} %get-tuple-element.11.m), custom_call_target="tpu_custom_call" | custom-call | tf_op jit(solution)/shard_map/pallas_call | solution.py:568

commit v6 on v5

--- a/solution.py
+++ b/solution.py
@@ -82,8 +82,8 @@
         pltpu.make_async_copy(bound_h, tv_bound, local.at[8]),
         pltpu.make_async_copy(clip_h, clip_bound, local.at[9]),
     ]
-    for copy in fetch:
-        copy.start()
+    for n in (4, 0, 1, 5, 6, 7, 8, 9):
+        fetch[n].start()
 
     lane = lax.broadcasted_iota(jnp.int32, (1, ncol), 1)
     group_bit = [(lane // (cols << b)) % 2 == 0 for b in range(3)]
@@ -174,6 +174,8 @@
     pl.semaphore_wait(barrier, len(peers))
     for copy in first:
         copy.start()
+    for n in (2, 3):
+        fetch[n].start()
 
     jac_n[images * rows:, :] = jnp.zeros((jac_n.shape[0] - images * rows, ncol), F32)
     jac_hn[images * HALO:, :] = jnp.zeros((jac_hn.shape[0] - images * HALO, ncol), F32)

time: 27.6 us -> 27.7 us (level)
  no operation moved by 1% of the time
where the time goes in v6:
time: 27.7 us; the launch traced here: 27.5 us
  Pallas kernels  24.3 us (88%)
  between operations  3.22 us (12%)
    pallas_call x1, Pallas kernels, per_device(): pl.pallas_call(functools.partial(kernel, tiles, waves, total_count), out_...  23.5 us
    pallas_call x1, Pallas kernels, per_device(): pl.pallas_call(hand_out, out_shape=(jax.ShapeDtypeStruct((npar, rows, nco...  0.72 us

profile of v6, /device:TPU:0, one launch (start us, length us, event | category | flops | bytes accessed | tf_op | source)
XLA Modules:
  0.0 27.5 jit_solution(10091317354421127895)
XLA Ops:
  3.2 23.5 %shard_map.121 = (f32[9,16,128]{2,1,0:T(8,128)S(1)}, f32[2,9,16,128]{3,2,1,0:T(8,128)S(1)}, f32[8,128]{1,0:T(8,128)S(1)}) custom-call(f32[9,16,128]{2,1,0:T(8,128)} %params_h.1, f32[2,9,16,128]{3,2,1,0:T(8,128)} %dual_h.1, bf16[36,16,128]{2,1,0:T(8,128)(2,1)} %bitcast.12, bf16[128,16,128]{2,1,0:T(8,128)(2,1)} %bitcast.11, f32[9,32]{1,0:T(8,128)} %response_h.1, ...), custom_call_target="tpu_custom_call" | custom-call | tf_op jit(solution)/shard_map/pallas_call | solution.py:491
  26.8 0.7 %shard_map.122 = (f32[9,16,128]{2,1,0:T(8,128)}, f32[2,9,16,128]{3,2,1,0:T(8,128)}, f32[1]{0:T(128)}) custom-call(f32[9,16,128]{2,1,0:T(8,128)S(1)} %get-tuple-element.9.x, f32[2,9,16,128]{3,2,1,0:T(8,128)S(1)} %get-tuple-element.10.d, f32[8,128]{1,0:T(8,128)S(1)} %get-tuple-element.11.m), custom_call_target="tpu_custom_call" | custom-call | tf_op jit(solution)/shard_map/pallas_call | solution.py:570
